TPU v7x, 32 devices: a whole 2x2x4 slice. The times are simulated.
32 devices in a mesh: brick: 8 (over z, x), region: 4 (over y, core).
Axes of the slice: x: 2, y: 2, z: 4, core: 2. Of those that a mesh axis runs over, the one named last changes fastest.
Arguments:
- segments: float32 [1024, 8, 128], P(('brick', 'region'))
- ship_list: int32 [32, 8, 4], P(('brick', 'region')), may hold values from 0 to 31
- kept_tiles: int32 [32, 64, 2], P(('brick', 'region')), may hold values from 0 to 63
- kept_count: int32 [32], P(('brick', 'region')), may hold values from 1 to 64, as said below
- lent_tiles: int32 [32, 4, 8, 2], P(('brick', 'region')), may hold values from 0 to 63
- lent_count: int32 [8, 4, 4], P('brick'), may hold values from 0 to 8, as said below
Outputs:
- loads: float32 [1024, 6, 128], P(('brick', 'region'))
Inputs may be any that keep to these rules, and one draw needn't show every extreme that they name: `kept_count`: in every brick one device has exactly 64 live kept slots. `lent_count`: zero where i equals j; in every brick some entry equals 8.
All inputs are finite; a program needn't handle non-finite values.
Results may differ from a plain program's by a relative error of at most 0.0001.
Values sent between devices are 32-bit elements; how exact they have to be, the bound alone decides.
No kernel may reach another device: no remote copies, remote signals or barrier semaphores. Data moves between devices by JAX's collectives and lax.ppermute only.
A program may use at most 64 MiB of HBM per device.

v0:
```python
import jax
import jax.numpy as jnp
from jax import lax
from jax.experimental import pallas as pl
from jax.experimental.pallas import tpu as pltpu
from jax.sharding import PartitionSpec as P

DIST_FLOOR = 0.0025
PARALLEL_FLOOR = 0.05
TINY = 1e-20
STAND_IN = 1e-30
SHIFT = 10
F32 = jnp.float32
BF16 = jnp.bfloat16

GROUPS = 12
DEPTH = 8 * GROUPS
RIGHT_ROWS = 8 * (3 * 6 + 7 * 4)
OUTS = 13
PLACES = [{0: 3 * n, 1: 3 * n + 1, 2: 3 * n + 2} for n in range(3)] + [{}, {}, {}, {}, {}, {}]
for _n in range(7):
    PLACES[2 + _n].update({4: 9 + 2 * _n, 5: 10 + 2 * _n})
PLACES += [{}] * 4
HEAD = 8
BATCH = 4
PREP = 8


def parts(x):
    first = x.astype(BF16).astype(F32)
    rest = x - first
    second = rest.astype(BF16).astype(F32)
    return first, second, rest - second


def write_blocks(src, feat, left, right, first, blocks):
    row = lax.broadcasted_iota(jnp.int32, (8, 128), 0)
    is_dir = (row >= 3) & (row < 6)
    one = jnp.ones((8, 128), F32)
    zero = jnp.zeros((8, 128), F32)

    def pick(mask, x):
        return jnp.where(mask, x, 0.0)

    def total(x):
        return jnp.broadcast_to(jnp.sum(x, axis=0, keepdims=True), (8, 128))

    def spread(x, r):
        return jnp.broadcast_to(x[r : r + 1, :], (8, 128))

    def one_block(n):
        x = src[pl.ds(pl.multiple_of(n * 8, 8), 8), :]
        squared = total(pick(is_dir, x * x))
        inverse = lax.rsqrt(squared)
        pose = jnp.where(is_dir, x * inverse, pick(row < 3, x))
        along = total(pick(is_dir, pose * pltpu.roll(pose, 3, 0)))
        length = squared * inverse
        flipped = 1.0 / jnp.where(x == 0.0, STAND_IN, x)
        single = pick(row == 4, length)
        for r, value in ((3, spread(flipped, 6)), (2, 0.75 * spread(flipped, 7)), (1, spread(x, 6)), (0, along)):
            single = jnp.where(row == r, value, single)
        at = first + n
        feat[pl.ds(pl.multiple_of(at * 8, 8), 8), :] = jnp.where(row == 3, length, pltpu.roll(pose, 5, 0))
        p, q = parts(pose), parts(single)
        stack = jnp.concatenate([p[0], p[0], p[0], p[1], p[1], p[2], *q, one, one, one], axis=0)
        left[pl.ds(pl.multiple_of(at * 128, 128), 128), 0:DEPTH] = jnp.transpose(stack.astype(BF16))
        halves = []
        for three in (
            [pick(is_dir, y) for y in p],
            [pick(is_dir, -pltpu.roll(y, 3, 0)) for y in p],
            [pick(row < 3, pltpu.roll(y, 5, 0)) for y in p],
        ):
            halves += [three[m] for m in (0, 1, 2, 0, 1, 0)]
        for source, r in ((q, 0), (p, 0), (p, 1), (p, 2)):
            halves += [zero] + [pick(row == r, -y) for y in source]
        for r in (1, 2, 3):
            halves += [jnp.where(row == r, 1.0, 0.0)] + [pick(row == r, y) for y in q]
        right[pl.ds(pl.multiple_of(at * RIGHT_ROWS, 16), RIGHT_ROWS), :] = jnp.concatenate(halves, axis=0).astype(BF16)

    def step(n, carry):
        for u in range(PREP):
            one_block(n * PREP + u)
        return carry

    lax.fori_loop(0, blocks // PREP, step, 0)


def write_template(fixed):
    row = lax.broadcasted_iota(jnp.int32, (DEPTH, 128), 0)
    picks = [[], [48, 56, 64], []]
    picks += [[k, 24 + k, 40 + k] for k in range(3)]
    picks += [[48 + n, 56 + n, 64 + n] for n in (1, 2, 3)]
    picks += [[3 + k, 27 + k, 43 + k] for k in range(3)]
    picks += [[52, 60, 68]]
    for n, chosen in enumerate(picks):
        hit = jnp.zeros((DEPTH, 128), jnp.bool_)
        for r in chosen:
            hit = hit | (row == r)
        fixed[:, 128 * n : 128 * (n + 1)] = jnp.where(hit, 1.0, 0.0).astype(BF16)


def products(left, right, fixed, prod, pair):
    ia, ib = pair
    a = left[pl.ds(pl.multiple_of(ia * 128, 128), 128), 0:DEPTH]
    mine = right[pl.ds(pl.multiple_of(ib * RIGHT_ROWS, 16), RIGHT_ROWS), :]

    def column(n):
        places = PLACES[n]
        rows = []
        for k in range(GROUPS // 2):
            if k in places:
                rows.append(mine[16 * places[k] : 16 * places[k] + 16, :])
            else:
                rows.append(fixed[16 * k : 16 * k + 16, 128 * n : 128 * (n + 1)])
        return jnp.concatenate(rows, axis=0)

    for low in range(0, OUTS, 2):
        high = min(low + 2, OUTS)
        b = jnp.concatenate([column(n) for n in range(low, high)], axis=1)
        prod[:, 128 * low : 128 * high] = lax.dot_general(
            a, b, (((1,), (0,)), ((), ())), preferred_element_type=F32
        )


def pair_sums(feat, prod, part, ib):
    ux2, uy2, uz2, len2 = (jnp.broadcast_to(feat[pl.ds(ib * 8 + q, 1), :], (8, 128)) for q in range(4))
    sums = None
    for g in range(16):
        rows = slice(8 * g, 8 * g + 8)
        w, c, f, ox, oy, oz, reach, compliance, curvature, ux1, uy1, uz1, len1 = (
            prod[rows, 128 * n : 128 * (n + 1)] for n in range(OUTS)
        )
        inverse = pl.reciprocal(jnp.maximum(1.0 - w * w, PARALLEL_FLOOR))
        s = jnp.minimum(jnp.maximum((w * f - c) * inverse, 0.0), len1)
        t = jnp.minimum(jnp.maximum(w * s + f, 0.0), len2)
        s = jnp.minimum(jnp.maximum(w * t - c, 0.0), len1)
        gx = ox + s * ux1 - t * ux2
        gy = oy + s * uy1 - t * uy2
        gz = oz + s * uz1 - t * uz2
        square = jnp.maximum(gx * gx + gy * gy + gz * gz, DIST_FLOOR)
        near = lax.rsqrt(square)
        depth = jnp.maximum(reach - square * near, TINY)
        root = lax.rsqrt(depth * curvature)
        scale = (depth * root) * (depth * near) * pl.reciprocal(compliance)
        force = [scale * gx, scale * gy, scale * gz]
        on_a = force + [s * x for x in force]
        on_b = force + [t * x for x in force]
        for q in range(6):
            part[rows, q : q + 1] = jnp.sum(on_a[q], axis=1, keepdims=True)
        sums = on_b if sums is None else [x + y for x, y in zip(sums, on_b)]
    return jnp.concatenate([jnp.sum(x, axis=0, keepdims=True) for x in sums] + [jnp.zeros((2, 128), F32)], axis=0)


def block_arrays(blocks):
    return [
        pltpu.VMEM((blocks * 8, 128), F32),
        pltpu.VMEM((blocks * 128, 128), BF16),
        pltpu.VMEM((blocks * RIGHT_ROWS, 128), BF16),
    ]


def tile_scratch():
    return [
        pltpu.VMEM((DEPTH, OUTS * 128), BF16),
        *[pltpu.VMEM((128, OUTS * 128), F32)] * (2 * BATCH),
        *[pltpu.VMEM((128, 128), F32)] * (2 * BATCH),
        *[pltpu.VMEM((8, 128), F32)] * (2 * BATCH),
    ]


def run_tiles(blocks, scratch, acc, code_at, count):
    feat, left, right = blocks
    fixed = scratch[0]
    prods, sums_a, sums_b = (scratch[1 + 2 * BATCH * k : 1 + 2 * BATCH * (k + 1)] for k in range(3))
    write_template(fixed)
    for ref in (*sums_a, *sums_b):
        ref[...] = jnp.zeros_like(ref)

    def ids(n):
        code = code_at(n)
        return lax.shift_right_logical(code, SHIFT), code & ((1 << SHIFT) - 1)

    def collect(first, side):
        for u in range(BATCH):
            ia, ib = ids(jnp.maximum(first + u, 0))
            slot = side * BATCH + u
            acc[pl.ds(pl.multiple_of(ia * 8, 8), 8), :] += jnp.transpose(sums_a[slot][...])[0:8, :]
            acc[pl.ds(pl.multiple_of(ib * 8, 8), 8), :] -= sums_b[slot][...]

    def prepare(first, side):
        for u in range(BATCH):
            products(left, right, fixed, prods[side * BATCH + u], ids(first + u))

    def batch(first, side):
        collect(first - BATCH, 1 - side)
        prepare(first + BATCH, 1 - side)
        for u in range(BATCH):
            slot = side * BATCH + u
            sums_b[slot][...] = pair_sums(feat, prods[slot], sums_a[slot], ids(first + u)[1])

    prepare(0, 0)

    def step(n, carry):
        first = 2 * BATCH * n
        batch(first, 0)

        @pl.when(first + BATCH < count)
        def _():
            batch(first + BATCH, 1)

        return carry

    lax.fori_loop(0, (count + 2 * BATCH - 1) // (2 * BATCH), step, 0)
    batches = (count + BATCH - 1) // BATCH

    @pl.when((batches & 1) == 1)
    def _():
        collect((batches - 1) * BATCH, 0)

    @pl.when((batches > 0) & ((batches & 1) == 0))
    def _():
        collect((batches - 1) * BATCH, 1)


def gather_kernel(ship_ref, seg_ref, out_ref):
    slots, bricks = ship_ref.shape[1:]
    for q in range(bricks):
        for k in range(slots):
            out_ref[q, 8 * k : 8 * k + 8, :] = seg_ref[pl.ds(pl.multiple_of(ship_ref[0, k, q] * 8, 8), 8), :]


def plan_kernel(ship_ref, kept_ref, count_ref, lent_ref, plan_ref, seg_ref, list_ref, near_ref):
    slots, bricks = ship_ref.shape[1:]
    peers = lent_ref.shape[1]
    leaves = seg_ref.shape[0] // 8
    brick = lax.axis_index("brick")
    region = lax.axis_index("region")
    mine = leaves + brick * slots

    def local_id(e):
        ghost = e - mine
        is_mine = (ghost >= 0) & (ghost < slots)
        return jnp.where(is_mine, ship_ref[0, jnp.where(is_mine, ghost, 0), brick], e)

    def file_tile(a, b, carry):
        near, far = carry
        a, b = local_id(a), local_id(b)
        code = lax.shift_left(a, SHIFT) | b
        is_near = (a < leaves) & (b < leaves)
        near_ref[near] = code
        list_ref[HEAD + far] = code
        step = is_near.astype(jnp.int32)
        return near + step, far + 1 - step

    carry = lax.fori_loop(
        0, count_ref[0], lambda k, c: file_tile(kept_ref[0, 0, k], kept_ref[0, 1, k], c), (0, 0)
    )
    for j in range(peers):
        carry = lax.fori_loop(
            0, plan_ref[0, region, j], lambda k, c: file_tile(lent_ref[0, j, 0, k], lent_ref[0, j, 1, k], c), carry
        )
    near, far = carry

    def append(k, carry):
        list_ref[HEAD + far + k] = near_ref[k]
        return carry

    lax.fori_loop(0, near, append, 0)
    list_ref[0] = near + far
    list_ref[1] = near


def tile_kernel(list_ref, other_ref, seg_ref, ghost_ref, guest_ref, own_ref, back_ref, loan_ref, acc, feat, left, right, *scratch):
    own_rows = seg_ref.shape[0]
    leaves = own_rows // 8
    ghosts = ghost_ref.shape[0] // 8
    ext = leaves + ghosts
    bricks = back_ref.shape[0]
    slots = ghosts // bricks
    last = list_ref.shape[0] - 1
    excess = list_ref[0] - other_ref[0]
    give = jnp.minimum(lax.shift_right_arithmetic(jnp.maximum(excess, 0), 1), list_ref[1])
    take = jnp.minimum(lax.shift_right_arithmetic(jnp.maximum(-excess, 0), 1), other_ref[1])
    keep = list_ref[0] - give
    borrowed = HEAD + other_ref[0] - take - keep
    guest_code = (ext << SHIFT) | ext
    dummy_code = ((ext + leaves) << SHIFT) | (ext + leaves)

    def code_at(n):
        kept = list_ref[jnp.minimum(HEAD + n, last)]
        lent = other_ref[jnp.clip(borrowed + n, 0, last)] + guest_code
        return jnp.where(n < keep, kept, jnp.where(n < keep + take, lent, dummy_code))

    acc[...] = jnp.zeros_like(acc)
    write_blocks(seg_ref, feat, left, right, 0, leaves)
    write_blocks(ghost_ref, feat, left, right, leaves, ghosts)

    @pl.when(take > 0)
    def _():
        write_blocks(guest_ref, feat, left, right, ext, leaves)

    run_tiles((feat, left, right), scratch, acc, code_at, keep + take)
    own_ref[...] = acc[0:own_rows, :]
    loan_ref[...] = acc[8 * ext : 8 * ext + own_rows, :]
    for q in range(bricks):
        for k in range(slots):
            row = own_rows + 8 * (q * slots + k)
            back_ref[q, 6 * k : 6 * k + 6, :] = acc[row : row + 6, :]


def stride_rows(first, count, row, stride):
    return pl.ds(first * stride + row, count, stride=stride)


def finish_kernel(ship_ref, seg_ref, own_ref, loan_ref, back_ref, out_ref, acc):
    leaves = seg_ref.shape[0] // 8
    slots, bricks = ship_ref.shape[1:]
    acc[...] = own_ref[...] + loan_ref[...]
    for q in range(bricks):
        for k in range(slots):
            row = pl.multiple_of(ship_ref[0, k, q] * 8, 8)
            acc[pl.ds(row, 6), :] += back_ref[q, 6 * k : 6 * k + 6, :]
    for c in range(0, leaves, 8):
        d = [seg_ref[stride_rows(c, 8, 3 + q, 8), :] for q in range(3)]
        force = [acc[stride_rows(c, 8, q, 8), :] for q in range(3)]
        lever = [acc[stride_rows(c, 8, 3 + q, 8), :] for q in range(3)]
        squared = d[0] * d[0] + d[1] * d[1] + d[2] * d[2]
        inverse = lax.rsqrt(squared)
        half = 0.5 * squared * inverse
        unit = [x * inverse for x in d]
        m = [x - half * y for x, y in zip(lever, force)]
        for q in range(3):
            i, j = (q + 1) % 3, (q + 2) % 3
            out_ref[q, c : c + 8, :] = force[q]
            out_ref[3 + q, c : c + 8, :] = unit[i] * m[j] - unit[j] * m[i]


def body(segments, ship_list, kept_tiles, kept_count, lent_tiles, lent_count):
    leaves = segments.shape[0]
    bricks, slots = ship_list.shape[1:]
    keep = kept_tiles.shape[1]
    peers, lend = lent_tiles.shape[1:3]
    ghosts = bricks * slots
    ext = leaves + ghosts
    cap = -(-(HEAD + keep + peers * lend + 1) // 128) * 128
    ship = jnp.transpose(ship_list, (0, 2, 1))
    kept = jnp.transpose(kept_tiles, (0, 2, 1))
    lent = jnp.transpose(lent_tiles, (0, 1, 3, 2))
    flat = segments.reshape(leaves * 8, 128)
    smem = pl.BlockSpec(memory_space=pltpu.SMEM)
    vmem = pl.BlockSpec(memory_space=pltpu.VMEM)
    tile_list = jax.ShapeDtypeStruct((cap,), jnp.int32)
    own_sums = jax.ShapeDtypeStruct((leaves * 8, 128), F32)

    def on_chip(x):
        return pltpu.with_memory_space_constraint(x, pltpu.VMEM)

    outgoing = pl.pallas_call(
        gather_kernel,
        out_shape=jax.ShapeDtypeStruct((bricks, slots * 8, 128), F32),
        in_specs=[smem, vmem],
        out_specs=vmem,
        name="ship_gather",
    )(ship, flat)
    incoming = lax.all_to_all(outgoing, "brick", split_axis=0, concat_axis=0, tiled=True)
    partner = [(r, r ^ 1) for r in range(lax.axis_size("region"))]
    guests = lax.ppermute(flat, "region", partner)
    tiles = pl.pallas_call(
        plan_kernel,
        out_shape=tile_list,
        in_specs=[smem] * 5 + [pl.BlockSpec(memory_space=pl.ANY)],
        out_specs=smem,
        scratch_shapes=[pltpu.SMEM((cap,), jnp.int32)],
        name="plan_tiles",
    )(ship, kept, kept_count, lent, lent_count, flat)
    other_tiles = lax.ppermute(tiles, "region", partner)
    own, back, loan = pl.pallas_call(
        tile_kernel,
        out_shape=[own_sums, jax.ShapeDtypeStruct((bricks, slots * 6, 128), F32), own_sums],
        in_specs=[smem, smem, vmem, vmem, vmem],
        out_specs=[vmem, vmem, vmem],
        scratch_shapes=[
            pltpu.VMEM(((ext + leaves + 1) * 8, 128), F32),
            *block_arrays(ext + leaves + 1),
            *tile_scratch(),
        ],
        name="all_tiles",
    )(tiles, other_tiles, flat, on_chip(incoming.reshape(ghosts * 8, 128)), on_chip(guests))
    repaid = lax.ppermute(loan, "region", partner)
    returned = lax.all_to_all(back, "brick", split_axis=0, concat_axis=0, tiled=True)
    loads = pl.pallas_call(
        finish_kernel,
        out_shape=jax.ShapeDtypeStruct((6, leaves, 128), F32),
        in_specs=[smem, vmem, vmem, vmem, vmem],
        out_specs=vmem,
        scratch_shapes=[pltpu.VMEM((leaves * 8, 128), F32)],
        name="finish",
    )(ship, flat, own, on_chip(repaid), on_chip(returned))
    return jnp.transpose(loads, (1, 0, 2))


def solution(mesh):
    placed = (
        P(("brick", "region"), None, None),
        P(("brick", "region"), None, None),
        P(("brick", "region"), None, None),
        P(("brick", "region")),
        P(("brick", "region"), None, None, None),
        P("brick", None, None),
    )
    return jax.shard_map(
        body,
        mesh=mesh,
        in_specs=placed,
        out_specs=P(("brick", "region"), None, None),
        check_vma=False,
    )
```

profile of v0, /device:TPU:0, one launch (start us, length us, event | category | flops | bytes accessed | tf_op | source)
XLA Modules:
  0.0 47.2 jit_solution(15756449597373425743)
XLA Ops:
  0.0 1.6 %ship_gather.1 = f32[8,32,128]{2,1,0:T(8,128)} custom-call(s32[1,4,8]{2,1,0:T(4,128)} %bitcast.12, f32[256,128]{1,0:T(8,128)} %bitcast.7), custom_call_target="tpu_custom_call" | custom-call | tf_op jit(solution)/shard_map/ship_gather/pallas_call | solution.py:358
  1.6 0.0 copy-start
  1.6 7.4 %all-to-all-start = ((f32[8,32,128]{2,1,0:T(8,128)}), f32[8,32,128]{2,1,0:T(8,128)S(1)}, u32[]{:S(2)}, u32[]{:S(2)}) async-start(f32[8,32,128]{2,1,0:T(8,128)} %ship_gather.1), calls=%async_computation | async-start | bytes 262144 | tf_op jit(solution)/shard_map/all_to_all | solution.py:365
  9.0 0.0 copy-done
  9.0 0.1 collective-permute-start.1
  9.7 2.3 %plan_tiles.1.list_ref = s32[128]{0:T(128)} custom-call(s32[1,4,8]{2,1,0:T(4,128)} %bitcast.13, s32[1,2,64]{2,1,0:T(2,128)} %bitcast.16, s32[1]{0:T(128)S(6)} %copy.7.count_ref, s32[1,4,2,8]{3,2,1,0:T(2,128)} %bitcast.15, s32[1,4,4]{2,1,0:T(4,128)} %plan_ref.1, f32[256,128]{1,0:T(8,128)} %bitcast.8), custom_call_target="tpu_custom_call" | custom-call | tf_op jit(solution)/shard_map/plan_tiles/pallas_call | solution.py:368
  12.0 1.2 %collective-permute-start = (s32[128]{0:T(128)}, s32[128]{0:T(128)S(1)}, u32[]{:S(2)}, u32[]{:S(2)}) collective-permute-start(s32[128]{0:T(128)} %plan_tiles.1.list_ref), channel_id=1, source_target_pairs={{0,1},{1,0},{2,3},{3,2},{4,5},{5,4},{6,7},{7,6},{8,9},{9,8},{10,11... | collective-permute-start | bytes 1544 | tf_op jit(solution)/shard_map/ppermute | solution.py:376
  13.2 1.0 %collective-permute-done.other_ref = s32[128]{0:T(128)S(1)} collective-permute-done((s32[128]{0:T(128)}, s32[128]{0:T(128)S(1)}, u32[]{:S(2)}, u32[]{:S(2)}) %collective-permute-start) | collective-permute-done | bytes 544 | tf_op jit(solution)/shard_map/ppermute | solution.py:376
  14.3 0.0 copy-start.1
  14.3 0.0 collective-permute-done.1.guest_ref
  14.3 2.1 %all-to-all-done = f32[8,32,128]{2,1,0:T(8,128)S(1)} async-done(((f32[8,32,128]{2,1,0:T(8,128)}), f32[8,32,128]{2,1,0:T(8,128)S(1)}, u32[]{:S(2)}, u32[]{:S(2)}) %all-to-all-start) | async-done | bytes 131104 | tf_op jit(solution)/shard_map/all_to_all | solution.py:365
  16.3 0.0 copy-done.1
  16.3 18.5 %all_tiles.1 = (f32[256,128]{1,0:T(8,128)}, f32[8,24,128]{2,1,0:T(8,128)}, f32[256,128]{1,0:T(8,128)}) custom-call(s32[128]{0:T(128)} %plan_tiles.1.list_ref, s32[128]{0:T(128)} %copy-done.1, f32[256,128]{1,0:T(8,128)} %bitcast.9, f32[256,128]{1,0:T(8,128)S(1)} %bitcast.6, f32[256,128]{1,0:T(8,128)S(1)} %collective-permute-done.1.guest_ref), custom_call_target="tpu_custom_call" | custom-call | tf_op jit(solution)/shard_map/all_tiles/pallas_call | solution.py:377
  34.8 0.0 copy-start.2
  34.8 3.5 %all-to-all-start.1 = ((f32[8,24,128]{2,1,0:T(8,128)}), f32[8,24,128]{2,1,0:T(8,128)S(1)}, u32[]{:S(2)}, u32[]{:S(2)}) async-start(f32[8,24,128]{2,1,0:T(8,128)} %get-tuple-element.10), calls=%async_computation.1 | async-start | bytes 196608 | tf_op jit(solution)/shard_map/all_to_all | solution.py:390
  38.3 0.0 copy-done.2
  38.3 0.1 collective-permute-start.2
  38.4 1.3 %collective-permute-done.2.loan_ref = f32[256,128]{1,0:T(8,128)S(1)} collective-permute-done((f32[256,128]{1,0:T(8,128)S(1)}, f32[256,128]{1,0:T(8,128)S(1)}, u32[]{:S(2)}, u32[]{:S(2)}) %collective-permute-start.2) | collective-permute-done | bytes 131104 | tf_op jit(solution)/shard_map/ppermute | solution.py:389
  39.8 5.6 %all-to-all-done.1.back_ref = f32[8,24,128]{2,1,0:T(8,128)S(1)} async-done(((f32[8,24,128]{2,1,0:T(8,128)}), f32[8,24,128]{2,1,0:T(8,128)S(1)}, u32[]{:S(2)}, u32[]{:S(2)}) %all-to-all-start.1) | async-done | bytes 98336 | tf_op jit(solution)/shard_map/all_to_all | solution.py:390
  45.4 1.8 %finish.1 = f32[6,32,128]{2,1,0:T(8,128)} custom-call(s32[1,4,8]{2,1,0:T(4,128)} %bitcast.14, f32[256,128]{1,0:T(8,128)} %bitcast.10, f32[256,128]{1,0:T(8,128)} %get-tuple-element.8.own_ref, f32[256,128]{1,0:T(8,128)S(1)} %collective-permute-done.2.loan_ref, f32[8,24,128]{2,1,0:T(8,128)S(1)} %all-to-all-done.1.back_ref), custom_call_target="tpu_custom_call" | custom-call | tf_op jit(solution)/shard_map/finish/pallas_call | solution.py:391
Async XLA Ops:
  1.6 7.4 %copy-start = (f32[32,8,128]{2,1,0:T(8,128)S(1)}, f32[32,8,128]{2,1,0:T(8,128)}, u32[]{:S(2)}) copy-start(f32[32,8,128]{2,1,0:T(8,128)} %param.6) | copy-start | bytes 393220
  1.6 14.8 %all-to-all-start = ((f32[8,32,128]{2,1,0:T(8,128)}), f32[8,32,128]{2,1,0:T(8,128)S(1)}, u32[]{:S(2)}, u32[]{:S(2)}) async-start(f32[8,32,128]{2,1,0:T(8,128)} %ship_gather.1), calls=%async_computation | async-start | bytes 262144 | tf_op jit(solution)/shard_map/all_to_all | solution.py:365
  9.0 5.3 %collective-permute-start.1 = (f32[256,128]{1,0:T(8,128)S(1)}, f32[256,128]{1,0:T(8,128)S(1)}, u32[]{:S(2)}, u32[]{:S(2)}) collective-permute-start(f32[256,128]{1,0:T(8,128)S(1)} %bitcast.11), channel_id=1, source_target_pairs={{0,1},{1,0},{2,3},{3,2},{4,5},{5,4},{6,7},{7,6},{8,9},{9,8},{10,11... | collective-permute-start | bytes 393224 | tf_op jit(solution)/shard_map/ppermute | solution.py:367
  12.0 2.2 %collective-permute-start = (s32[128]{0:T(128)}, s32[128]{0:T(128)S(1)}, u32[]{:S(2)}, u32[]{:S(2)}) collective-permute-start(s32[128]{0:T(128)} %plan_tiles.1.list_ref), channel_id=1, source_target_pairs={{0,1},{1,0},{2,3},{3,2},{4,5},{5,4},{6,7},{7,6},{8,9},{9,8},{10,11... | collective-permute-start | bytes 1544 | tf_op jit(solution)/shard_map/ppermute | solution.py:376
  14.3 2.1 %copy-start.1 = (s32[128]{0:T(128)}, s32[128]{0:T(128)S(1)}, u32[]{:S(2)}) copy-start(s32[128]{0:T(128)S(1)} %collective-permute-done.other_ref) | copy-start | bytes 1540
  34.8 3.5 %copy-start.2 = (f32[256,128]{1,0:T(8,128)S(1)}, f32[256,128]{1,0:T(8,128)}, u32[]{:S(2)}) copy-start(f32[256,128]{1,0:T(8,128)} %get-tuple-element.9) | copy-start | bytes 393220
  34.8 10.6 %all-to-all-start.1 = ((f32[8,24,128]{2,1,0:T(8,128)}), f32[8,24,128]{2,1,0:T(8,128)S(1)}, u32[]{:S(2)}, u32[]{:S(2)}) async-start(f32[8,24,128]{2,1,0:T(8,128)} %get-tuple-element.10), calls=%async_computation.1 | async-start | bytes 196608 | tf_op jit(solution)/shard_map/all_to_all | solution.py:390
  38.3 1.4 %collective-permute-start.2 = (f32[256,128]{1,0:T(8,128)S(1)}, f32[256,128]{1,0:T(8,128)S(1)}, u32[]{:S(2)}, u32[]{:S(2)}) collective-permute-start(f32[256,128]{1,0:T(8,128)S(1)} %copy-done.2), channel_id=1, source_target_pairs={{0,1},{1,0},{2,3},{3,2},{4,5},{5,4},{6,7},{7,6},{8,9},{9,8},{10,11... | collective-permute-start | bytes 393224 | tf_op jit(solution)/shard_map/ppermute | solution.py:389
where the time goes:
time: 47 us; the launch traced here: 47.2 us
  Pallas kernels  24.2 us (51%)
  starting transfers between devices  12.2 us (26%)
  waiting for transfers between devices  10.1 us (21%)
  between operations  0.7 us (1%)
    pallas_call x1, Pallas kernels, body(): pl.pallas_call(tile_kernel, out_shape=[own_sums, jax.ShapeDtypeStruct((br...  18.5 us
    all_to_all x1, starting transfers between devices, body(): lax.all_to_all(outgoing, 'brick', split_axis=0, concat_axis=0, tiled=True)  7.41 us
    all_to_all x1, waiting for transfers between devices, body(): lax.all_to_all(back, 'brick', split_axis=0, concat_axis=0, tiled=True)  5.64 us
    all_to_all x1, starting transfers between devices, body(): lax.all_to_all(back, 'brick', split_axis=0, concat_axis=0, tiled=True)  3.49 us
    pallas_call x1, Pallas kernels, body(): pl.pallas_call(plan_kernel, out_shape=tile_list, in_specs=[smem] * 5 + [p...  2.3 us
    all_to_all x1, waiting for transfers between devices, body(): lax.all_to_all(outgoing, 'brick', split_axis=0, concat_axis=0, tiled=True)  2.08 us
    pallas_call x1, Pallas kernels, body(): pl.pallas_call(finish_kernel, out_shape=jax.ShapeDtypeStruct((6, leaves,...  1.8 us
    pallas_call x1, Pallas kernels, body(): pl.pallas_call(gather_kernel, out_shape=jax.ShapeDtypeStruct((bricks, slo...  1.58 us
  transfers between devices with their start and end apart: 5, of which 4 were waited for; matrix products, arithmetic and copies ran while one was open for 0% of the time, Pallas kernels for 5%

commit v1 on v0

--- a/solution.py
+++ b/solution.py
@@ -1,3 +1,5 @@
+import functools
+
 import jax
 import jax.numpy as jnp
 from jax import lax
@@ -229,10 +231,9 @@
             out_ref[q, 8 * k : 8 * k + 8, :] = seg_ref[pl.ds(pl.multiple_of(ship_ref[0, k, q] * 8, 8), 8), :]
 
 
-def plan_kernel(ship_ref, kept_ref, count_ref, lent_ref, plan_ref, seg_ref, list_ref, near_ref):
+def plan_kernel(leaves, ship_ref, kept_ref, count_ref, lent_ref, plan_ref, list_ref, near_ref):
     slots, bricks = ship_ref.shape[1:]
     peers = lent_ref.shape[1]
-    leaves = seg_ref.shape[0] // 8
     brick = lax.axis_index("brick")
     region = lax.axis_index("region")
     mine = leaves + brick * slots
@@ -270,7 +271,9 @@
     list_ref[1] = near
 
 
-def tile_kernel(list_ref, other_ref, seg_ref, ghost_ref, guest_ref, own_ref, back_ref, loan_ref, acc, feat, left, right, *scratch):
+def tile_kernel(
+    list_ref, other_in, seg_ref, ghost_ref, guest_ref, own_ref, back_ref, loan_ref, other_ref, sem, acc, feat, left, right, *scratch
+):
     own_rows = seg_ref.shape[0]
     leaves = own_rows // 8
     ghosts = ghost_ref.shape[0] // 8
@@ -278,6 +281,12 @@
     bricks = back_ref.shape[0]
     slots = ghosts // bricks
     last = list_ref.shape[0] - 1
+    fetch = pltpu.make_async_copy(other_in, other_ref, sem)
+    fetch.start()
+    acc[...] = jnp.zeros_like(acc)
+    write_blocks(seg_ref, feat, left, right, 0, leaves)
+    write_blocks(ghost_ref, feat, left, right, leaves, ghosts)
+    fetch.wait()
     excess = list_ref[0] - other_ref[0]
     give = jnp.minimum(lax.shift_right_arithmetic(jnp.maximum(excess, 0), 1), list_ref[1])
     take = jnp.minimum(lax.shift_right_arithmetic(jnp.maximum(-excess, 0), 1), other_ref[1])
@@ -290,10 +299,6 @@
         kept = list_ref[jnp.minimum(HEAD + n, last)]
         lent = other_ref[jnp.clip(borrowed + n, 0, last)] + guest_code
         return jnp.where(n < keep, kept, jnp.where(n < keep + take, lent, dummy_code))
-
-    acc[...] = jnp.zeros_like(acc)
-    write_blocks(seg_ref, feat, left, right, 0, leaves)
-    write_blocks(ghost_ref, feat, left, right, leaves, ghosts)
 
     @pl.when(take > 0)
     def _():
@@ -366,26 +371,32 @@
     partner = [(r, r ^ 1) for r in range(lax.axis_size("region"))]
     guests = lax.ppermute(flat, "region", partner)
     tiles = pl.pallas_call(
-        plan_kernel,
+        functools.partial(plan_kernel, leaves),
         out_shape=tile_list,
-        in_specs=[smem] * 5 + [pl.BlockSpec(memory_space=pl.ANY)],
+        in_specs=[smem] * 5,
         out_specs=smem,
         scratch_shapes=[pltpu.SMEM((cap,), jnp.int32)],
         name="plan_tiles",
-    )(ship, kept, kept_count, lent, lent_count, flat)
+    )(ship, kept, kept_count, lent, lent_count)
     other_tiles = lax.ppermute(tiles, "region", partner)
     own, back, loan = pl.pallas_call(
         tile_kernel,
-        out_shape=[own_sums, jax.ShapeDtypeStruct((bricks, slots * 6, 128), F32), own_sums],
-        in_specs=[smem, smem, vmem, vmem, vmem],
+        out_shape=[
+            pltpu.VMEM(own_sums.shape, F32),
+            jax.ShapeDtypeStruct((bricks, slots * 6, 128), F32),
+            pltpu.VMEM(own_sums.shape, F32),
+        ],
+        in_specs=[smem, vmem, vmem, vmem, vmem],
         out_specs=[vmem, vmem, vmem],
         scratch_shapes=[
+            pltpu.SMEM((cap,), jnp.int32),
+            pltpu.SemaphoreType.DMA(()),
             pltpu.VMEM(((ext + leaves + 1) * 8, 128), F32),
             *block_arrays(ext + leaves + 1),
             *tile_scratch(),
         ],
         name="all_tiles",
-    )(tiles, other_tiles, flat, on_chip(incoming.reshape(ghosts * 8, 128)), on_chip(guests))
+    )(tiles, on_chip(other_tiles), on_chip(flat), on_chip(incoming.reshape(ghosts * 8, 128)), on_chip(guests))
     repaid = lax.ppermute(loan, "region", partner)
     returned = lax.all_to_all(back, "brick", split_axis=0, concat_axis=0, tiled=True)
     loads = pl.pallas_call(
@@ -395,7 +406,7 @@
         out_specs=vmem,
         scratch_shapes=[pltpu.VMEM((leaves * 8, 128), F32)],
         name="finish",
-    )(ship, flat, own, on_chip(repaid), on_chip(returned))
+    )(ship, on_chip(flat), on_chip(own), on_chip(repaid), on_chip(returned))
     return jnp.transpose(loads, (1, 0, 2))
 
 

time: 47 us -> 44.9 us (0.955); the launches traced: 47.2 us -> 44.2 us
  Pallas kernels: 24.2 us -> 21.5 us
  starting transfers between devices: 12.2 us -> 11.2 us
  waiting for transfers between devices: 10.1 us -> 10.8 us
    pallas_call x2, Pallas kernels: 20.8 us -> 18.5 us  [the longest x1 15.6 us: body(): pl.pallas_call(tile_kernel, out_shape=[pltpu.VMEM(own_sums.shape, F32), j...]
    ppermute x1, starting transfers between devices: 1.19 us -> 0.07 us  [body(): other_tiles = lax.ppermute(tiles, 'region', partner)]
  transfers between devices with their start and end apart: 5 -> 5, of which waited for: 4 -> 4; matrix products, arithmetic and copies ran while one was open for 0% -> 0% of each run, Pallas kernels for 5% -> 7%
where the time goes in v1:
time: 44.9 us; the launch traced here: 44.2 us
  Pallas kernels  21.5 us (48%)
  starting transfers between devices  11.2 us (25%)
  waiting for transfers between devices  10.8 us (24%)
  between operations  0.69 us (2%)
    pallas_call x1, Pallas kernels, body(): pl.pallas_call(tile_kernel, out_shape=[pltpu.VMEM(own_sums.shape, F32), j...  15.6 us
    all_to_all x1, starting transfers between devices, body(): lax.all_to_all(outgoing, 'brick', split_axis=0, concat_axis=0, tiled=True)  7.41 us
    all_to_all x1, waiting for transfers between devices, body(): lax.all_to_all(back, 'brick', split_axis=0, concat_axis=0, tiled=True)  5.78 us
    all_to_all x1, starting transfers between devices, body(): lax.all_to_all(back, 'brick', split_axis=0, concat_axis=0, tiled=True)  3.69 us
    pallas_call x1, Pallas kernels, body(): pl.pallas_call(functools.partial(plan_kernel, leaves), out_shape=tile_lis...  2.89 us
    all_to_all x1, waiting for transfers between devices, body(): lax.all_to_all(outgoing, 'brick', split_axis=0, concat_axis=0, tiled=True)  2.28 us
    pallas_call x1, Pallas kernels, body(): pl.pallas_call(gather_kernel, out_shape=jax.ShapeDtypeStruct((bricks, slo...  1.59 us
    pallas_call x1, Pallas kernels, body(): pl.pallas_call(finish_kernel, out_shape=jax.ShapeDtypeStruct((6, leaves,...  1.46 us
  transfers between devices with their start and end apart: 5, of which 4 were waited for; matrix products, arithmetic and copies ran while one was open for 0% of the time, Pallas kernels for 7%

profile of v1, /device:TPU:0, one launch (start us, length us, event | category | flops | bytes accessed | tf_op | source)
XLA Modules:
  0.0 44.2 jit_solution(4091340311661380945)
XLA Ops:
  0.0 1.6 %ship_gather.1 = f32[8,32,128]{2,1,0:T(8,128)} custom-call(s32[1,4,8]{2,1,0:T(4,128)} %bitcast.11, f32[256,128]{1,0:T(8,128)} %bitcast.6), custom_call_target="tpu_custom_call" | custom-call | tf_op jit(solution)/shard_map/ship_gather/pallas_call | solution.py:363
  1.6 0.0 copy-start
  1.6 7.4 %all-to-all-start = ((f32[8,32,128]{2,1,0:T(8,128)}), f32[8,32,128]{2,1,0:T(8,128)S(1)}, u32[]{:S(2)}, u32[]{:S(2)}) async-start(f32[8,32,128]{2,1,0:T(8,128)} %ship_gather.1), calls=%async_computation | async-start | bytes 262144 | tf_op jit(solution)/shard_map/all_to_all | solution.py:370
  9.0 0.0 copy-done
  9.0 0.1 collective-permute-start.1
  9.7 2.9 %plan_tiles.1.list_ref = s32[128]{0:T(128)} custom-call(s32[1,4,8]{2,1,0:T(4,128)} %bitcast.12, s32[1,2,64]{2,1,0:T(2,128)} %bitcast.15, s32[1]{0:T(128)S(6)} %copy.7.count_ref, s32[1,4,2,8]{3,2,1,0:T(2,128)} %bitcast.14, s32[1,4,4]{2,1,0:T(4,128)} %plan_ref.1), custom_call_target="tpu_custom_call" | custom-call | tf_op jit(solution)/shard_map/plan_tiles/pallas_call | solution.py:373
  12.6 0.1 collective-permute-start
  12.7 1.4 %collective-permute-done.other_in = s32[128]{0:T(128)S(1)} collective-permute-done((s32[128]{0:T(128)}, s32[128]{0:T(128)S(1)}, u32[]{:S(2)}, u32[]{:S(2)}) %collective-permute-start) | collective-permute-done | bytes 544 | tf_op jit(solution)/shard_map/ppermute | solution.py:381
  14.1 0.0 collective-permute-done.1.guest_ref
  14.1 2.3 %all-to-all-done = f32[8,32,128]{2,1,0:T(8,128)S(1)} async-done(((f32[8,32,128]{2,1,0:T(8,128)}), f32[8,32,128]{2,1,0:T(8,128)S(1)}, u32[]{:S(2)}, u32[]{:S(2)}) %all-to-all-start) | async-done | bytes 131104 | tf_op jit(solution)/shard_map/all_to_all | solution.py:370
  16.4 15.6 %all_tiles.1 = (f32[256,128]{1,0:T(8,128)S(1)}, f32[8,24,128]{2,1,0:T(8,128)}, f32[256,128]{1,0:T(8,128)S(1)}) custom-call(s32[128]{0:T(128)} %plan_tiles.1.list_ref, s32[128]{0:T(128)S(1)} %collective-permute-done.other_in, f32[256,128]{1,0:T(8,128)S(1)} %bitcast.8, f32[256,128]{1,0:T(8,128)S(1)} %bitcast.10, f32[256,128]{1,0:T(8,128)S(1)} %collective-permute-done.1.guest_ref), custom_call_target="tpu_custom_call" | custom-call | tf_op jit(solution)/shard_map/all_tiles/pallas_call | solution.py:382
  32.0 3.7 %all-to-all-start.1 = ((f32[8,24,128]{2,1,0:T(8,128)}), f32[8,24,128]{2,1,0:T(8,128)S(1)}, u32[]{:S(2)}, u32[]{:S(2)}) async-start(f32[8,24,128]{2,1,0:T(8,128)} %get-tuple-element.10), calls=%async_computation.1 | async-start | bytes 196608 | tf_op jit(solution)/shard_map/all_to_all | solution.py:401
  35.7 0.0 collective-permute-start.2
  35.7 1.3 %collective-permute-done.2.loan_ref = f32[256,128]{1,0:T(8,128)S(1)} collective-permute-done((f32[256,128]{1,0:T(8,128)S(1)}, f32[256,128]{1,0:T(8,128)S(1)}, u32[]{:S(2)}, u32[]{:S(2)}) %collective-permute-start.2) | collective-permute-done | bytes 131104 | tf_op jit(solution)/shard_map/ppermute | solution.py:400
  37.0 5.8 %all-to-all-done.1.back_ref = f32[8,24,128]{2,1,0:T(8,128)S(1)} async-done(((f32[8,24,128]{2,1,0:T(8,128)}), f32[8,24,128]{2,1,0:T(8,128)S(1)}, u32[]{:S(2)}, u32[]{:S(2)}) %all-to-all-start.1) | async-done | bytes 98336 | tf_op jit(solution)/shard_map/all_to_all | solution.py:401
  42.8 1.5 %finish.1 = f32[6,32,128]{2,1,0:T(8,128)} custom-call(s32[1,4,8]{2,1,0:T(4,128)} %bitcast.13, f32[256,128]{1,0:T(8,128)S(1)} %bitcast.9, f32[256,128]{1,0:T(8,128)S(1)} %get-tuple-element.8.own_ref, f32[256,128]{1,0:T(8,128)S(1)} %collective-permute-done.2.loan_ref, f32[8,24,128]{2,1,0:T(8,128)S(1)} %all-to-all-done.1.back_ref), custom_call_target="tpu_custom_call" | custom-call | tf_op jit(solution)/shard_map/finish/pallas_call | solution.py:402
Async XLA Ops:
  1.6 7.4 %copy-start = (f32[32,8,128]{2,1,0:T(8,128)S(1)}, f32[32,8,128]{2,1,0:T(8,128)}, u32[]{:S(2)}) copy-start(f32[32,8,128]{2,1,0:T(8,128)} %param.6) | copy-start | bytes 393220
  1.6 14.8 %all-to-all-start = ((f32[8,32,128]{2,1,0:T(8,128)}), f32[8,32,128]{2,1,0:T(8,128)S(1)}, u32[]{:S(2)}, u32[]{:S(2)}) async-start(f32[8,32,128]{2,1,0:T(8,128)} %ship_gather.1), calls=%async_computation | async-start | bytes 262144 | tf_op jit(solution)/shard_map/all_to_all | solution.py:370
  9.0 5.1 %collective-permute-start.1 = (f32[256,128]{1,0:T(8,128)S(1)}, f32[256,128]{1,0:T(8,128)S(1)}, u32[]{:S(2)}, u32[]{:S(2)}) collective-permute-start(f32[256,128]{1,0:T(8,128)S(1)} %bitcast.7), channel_id=1, source_target_pairs={{0,1},{1,0},{2,3},{3,2},{4,5},{5,4},{6,7},{7,6},{8,9},{9,8},{10,11... | collective-permute-start | bytes 393224 | tf_op jit(solution)/shard_map/ppermute | solution.py:372
  12.6 1.4 %collective-permute-start = (s32[128]{0:T(128)}, s32[128]{0:T(128)S(1)}, u32[]{:S(2)}, u32[]{:S(2)}) collective-permute-start(s32[128]{0:T(128)} %plan_tiles.1.list_ref), channel_id=1, source_target_pairs={{0,1},{1,0},{2,3},{3,2},{4,5},{5,4},{6,7},{7,6},{8,9},{9,8},{10,11... | collective-permute-start | bytes 1544 | tf_op jit(solution)/shard_map/ppermute | solution.py:381
  32.0 10.8 %all-to-all-start.1 = ((f32[8,24,128]{2,1,0:T(8,128)}), f32[8,24,128]{2,1,0:T(8,128)S(1)}, u32[]{:S(2)}, u32[]{:S(2)}) async-start(f32[8,24,128]{2,1,0:T(8,128)} %get-tuple-element.10), calls=%async_computation.1 | async-start | bytes 196608 | tf_op jit(solution)/shard_map/all_to_all | solution.py:401
  35.7 1.3 %collective-permute-start.2 = (f32[256,128]{1,0:T(8,128)S(1)}, f32[256,128]{1,0:T(8,128)S(1)}, u32[]{:S(2)}, u32[]{:S(2)}) collective-permute-start(f32[256,128]{1,0:T(8,128)S(1)} %get-tuple-element.9), channel_id=1, source_target_pairs={{0,1},{1,0},{2,3},{3,2},{4,5},{5,4},{6,7},{7,6},{8,9},{9,8},{10,11... | collective-permute-start | bytes 393224 | tf_op jit(solution)/shard_map/ppermute | solution.py:400

commit v2 on v1

--- a/solution.py
+++ b/solution.py
@@ -24,6 +24,7 @@
     PLACES[2 + _n].update({4: 9 + 2 * _n, 5: 10 + 2 * _n})
 PLACES += [{}] * 4
 HEAD = 8
+LOAN_COST = 3
 BATCH = 4
 PREP = 8
 
@@ -288,8 +289,8 @@
     write_blocks(ghost_ref, feat, left, right, leaves, ghosts)
     fetch.wait()
     excess = list_ref[0] - other_ref[0]
-    give = jnp.minimum(lax.shift_right_arithmetic(jnp.maximum(excess, 0), 1), list_ref[1])
-    take = jnp.minimum(lax.shift_right_arithmetic(jnp.maximum(-excess, 0), 1), other_ref[1])
+    give = jnp.minimum(lax.shift_right_arithmetic(jnp.maximum(excess - LOAN_COST, 0), 1), list_ref[1])
+    take = jnp.minimum(lax.shift_right_arithmetic(jnp.maximum(-excess - LOAN_COST, 0), 1), other_ref[1])
     keep = list_ref[0] - give
     borrowed = HEAD + other_ref[0] - take - keep
     guest_code = (ext << SHIFT) | ext
@@ -317,18 +318,25 @@
     return pl.ds(first * stride + row, count, stride=stride)
 
 
-def finish_kernel(ship_ref, seg_ref, own_ref, loan_ref, back_ref, out_ref, acc):
+def finish_kernel(ship_ref, seg_ref, own_ref, loan_ref, back_ref, out_ref, *accs):
     leaves = seg_ref.shape[0] // 8
     slots, bricks = ship_ref.shape[1:]
-    acc[...] = own_ref[...] + loan_ref[...]
+    for k, acc in enumerate(accs):
+        acc[...] = own_ref[...] if k == 0 else loan_ref[...] if k == 1 else jnp.zeros_like(acc)
     for q in range(bricks):
         for k in range(slots):
             row = pl.multiple_of(ship_ref[0, k, q] * 8, 8)
-            acc[pl.ds(row, 6), :] += back_ref[q, 6 * k : 6 * k + 6, :]
+            accs[k % len(accs)][pl.ds(row, 6), :] += back_ref[q, 6 * k : 6 * k + 6, :]
+
+    def summed(c, q):
+        rows = stride_rows(c, 8, q, 8)
+        first, second, third, fourth = (acc[rows, :] for acc in accs)
+        return (first + second) + (third + fourth)
+
     for c in range(0, leaves, 8):
         d = [seg_ref[stride_rows(c, 8, 3 + q, 8), :] for q in range(3)]
-        force = [acc[stride_rows(c, 8, q, 8), :] for q in range(3)]
-        lever = [acc[stride_rows(c, 8, 3 + q, 8), :] for q in range(3)]
+        force = [summed(c, q) for q in range(3)]
+        lever = [summed(c, 3 + q) for q in range(3)]
         squared = d[0] * d[0] + d[1] * d[1] + d[2] * d[2]
         inverse = lax.rsqrt(squared)
         half = 0.5 * squared * inverse
@@ -404,7 +412,7 @@
         out_shape=jax.ShapeDtypeStruct((6, leaves, 128), F32),
         in_specs=[smem, vmem, vmem, vmem, vmem],
         out_specs=vmem,
-        scratch_shapes=[pltpu.VMEM((leaves * 8, 128), F32)],
+        scratch_shapes=[pltpu.VMEM((leaves * 8, 128), F32)] * 4,
         name="finish",
     )(ship, on_chip(flat), on_chip(own), on_chip(repaid), on_chip(returned))
     return jnp.transpose(loads, (1, 0, 2))

time: 44.9 us -> 45.2 us (level)
  starting transfers between devices: 11.2 us -> 12.5 us
  waiting for transfers between devices: 10.8 us -> 10.1 us
    ppermute x1, starting transfers between devices: 0.07 us -> 1.59 us  [body(): other_tiles = lax.ppermute(tiles, 'region', partner)]
    pallas_call x1, Pallas kernels: 2.89 us -> 1.9 us  [body(): pl.pallas_call(functools.partial(plan_kernel, leaves), out_shape=tile_lis...]
    pallas_call x1, Pallas kernels: 15.6 us -> 16.5 us  [body(): pl.pallas_call(tile_kernel, out_shape=[pltpu.VMEM(own_sums.shape, F32), j...]
  transfers between devices with their start and end apart: 5 -> 5, of which waited for: 4 -> 4; matrix products, arithmetic and copies ran while one was open for 0% -> 0% of each run, Pallas kernels for 7% -> 4%
where the time goes in v2:
time: 45.2 us; the launch traced here: 44.8 us
  Pallas kernels  21.5 us (48%)
  starting transfers between devices  12.5 us (28%)
  waiting for transfers between devices  10.1 us (22%)
  between operations  0.7 us (2%)
    pallas_call x1, Pallas kernels, body(): pl.pallas_call(tile_kernel, out_shape=[pltpu.VMEM(own_sums.shape, F32), j...  16.5 us
    all_to_all x1, starting transfers between devices, body(): lax.all_to_all(outgoing, 'brick', split_axis=0, concat_axis=0, tiled=True)  7.41 us
    all_to_all x1, waiting for transfers between devices, body(): lax.all_to_all(back, 'brick', split_axis=0, concat_axis=0, tiled=True)  5.65 us
    all_to_all x1, starting transfers between devices, body(): lax.all_to_all(back, 'brick', split_axis=0, concat_axis=0, tiled=True)  3.37 us
    all_to_all x1, waiting for transfers between devices, body(): lax.all_to_all(outgoing, 'brick', split_axis=0, concat_axis=0, tiled=True)  2.09 us
    pallas_call x1, Pallas kernels, body(): pl.pallas_call(functools.partial(plan_kernel, leaves), out_shape=tile_lis...  1.9 us
    pallas_call x1, Pallas kernels, body(): pl.pallas_call(gather_kernel, out_shape=jax.ShapeDtypeStruct((bricks, slo...  1.59 us
    ppermute x1, starting transfers between devices, body(): other_tiles = lax.ppermute(tiles, 'region', partner)  1.59 us
  transfers between devices with their start and end apart: 5, of which 4 were waited for; matrix products, arithmetic and copies ran while one was open for 0% of the time, Pallas kernels for 4%

profile of v2, /device:TPU:0, one launch (start us, length us, event | category | flops | bytes accessed | tf_op | source)
XLA Modules:
  0.0 44.8 jit_solution(14499733226573259968)
XLA Ops:
  0.0 1.6 %ship_gather.1 = f32[8,32,128]{2,1,0:T(8,128)} custom-call(s32[1,4,8]{2,1,0:T(4,128)} %bitcast.11, f32[256,128]{1,0:T(8,128)} %bitcast.6), custom_call_target="tpu_custom_call" | custom-call | tf_op jit(solution)/shard_map/ship_gather/pallas_call | solution.py:371
  1.6 0.0 copy-start
  1.6 7.4 %all-to-all-start = ((f32[8,32,128]{2,1,0:T(8,128)}), f32[8,32,128]{2,1,0:T(8,128)S(1)}, u32[]{:S(2)}, u32[]{:S(2)}) async-start(f32[8,32,128]{2,1,0:T(8,128)} %ship_gather.1), calls=%async_computation | async-start | bytes 262144 | tf_op jit(solution)/shard_map/all_to_all | solution.py:378
  9.0 0.0 copy-done
  9.0 0.1 collective-permute-start.1
  9.7 1.9 %plan_tiles.1.list_ref = s32[128]{0:T(128)} custom-call(s32[1,4,8]{2,1,0:T(4,128)} %bitcast.12, s32[1,2,64]{2,1,0:T(2,128)} %bitcast.15, s32[1]{0:T(128)S(6)} %copy.7.count_ref, s32[1,4,2,8]{3,2,1,0:T(2,128)} %bitcast.14, s32[1,4,4]{2,1,0:T(4,128)} %plan_ref.1), custom_call_target="tpu_custom_call" | custom-call | tf_op jit(solution)/shard_map/plan_tiles/pallas_call | solution.py:381
  11.6 1.6 %collective-permute-start = (s32[128]{0:T(128)}, s32[128]{0:T(128)S(1)}, u32[]{:S(2)}, u32[]{:S(2)}) collective-permute-start(s32[128]{0:T(128)} %plan_tiles.1.list_ref), channel_id=1, source_target_pairs={{0,1},{1,0},{2,3},{3,2},{4,5},{5,4},{6,7},{7,6},{8,9},{9,8},{10,11... | collective-permute-start | bytes 1544 | tf_op jit(solution)/shard_map/ppermute | solution.py:389
  13.2 1.0 %collective-permute-done.other_in = s32[128]{0:T(128)S(1)} collective-permute-done((s32[128]{0:T(128)}, s32[128]{0:T(128)S(1)}, u32[]{:S(2)}, u32[]{:S(2)}) %collective-permute-start) | collective-permute-done | bytes 544 | tf_op jit(solution)/shard_map/ppermute | solution.py:389
  14.3 0.0 collective-permute-done.1.guest_ref
  14.3 2.1 %all-to-all-done = f32[8,32,128]{2,1,0:T(8,128)S(1)} async-done(((f32[8,32,128]{2,1,0:T(8,128)}), f32[8,32,128]{2,1,0:T(8,128)S(1)}, u32[]{:S(2)}, u32[]{:S(2)}) %all-to-all-start) | async-done | bytes 131104 | tf_op jit(solution)/shard_map/all_to_all | solution.py:378
  16.4 16.5 %all_tiles.1 = (f32[256,128]{1,0:T(8,128)S(1)}, f32[8,24,128]{2,1,0:T(8,128)}, f32[256,128]{1,0:T(8,128)S(1)}) custom-call(s32[128]{0:T(128)} %plan_tiles.1.list_ref, s32[128]{0:T(128)S(1)} %collective-permute-done.other_in, f32[256,128]{1,0:T(8,128)S(1)} %bitcast.8, f32[256,128]{1,0:T(8,128)S(1)} %bitcast.10, f32[256,128]{1,0:T(8,128)S(1)} %collective-permute-done.1.guest_ref), custom_call_target="tpu_custom_call" | custom-call | tf_op jit(solution)/shard_map/all_tiles/pallas_call | solution.py:390
  32.9 3.4 %all-to-all-start.1 = ((f32[8,24,128]{2,1,0:T(8,128)}), f32[8,24,128]{2,1,0:T(8,128)S(1)}, u32[]{:S(2)}, u32[]{:S(2)}) async-start(f32[8,24,128]{2,1,0:T(8,128)} %get-tuple-element.10), calls=%async_computation.1 | async-start | bytes 196608 | tf_op jit(solution)/shard_map/all_to_all | solution.py:409
  36.2 0.1 collective-permute-start.2
  36.3 1.3 %collective-permute-done.2.loan_ref = f32[256,128]{1,0:T(8,128)S(1)} collective-permute-done((f32[256,128]{1,0:T(8,128)S(1)}, f32[256,128]{1,0:T(8,128)S(1)}, u32[]{:S(2)}, u32[]{:S(2)}) %collective-permute-start.2) | collective-permute-done | bytes 131104 | tf_op jit(solution)/shard_map/ppermute | solution.py:408
  37.6 5.6 %all-to-all-done.1.back_ref = f32[8,24,128]{2,1,0:T(8,128)S(1)} async-done(((f32[8,24,128]{2,1,0:T(8,128)}), f32[8,24,128]{2,1,0:T(8,128)S(1)}, u32[]{:S(2)}, u32[]{:S(2)}) %all-to-all-start.1) | async-done | bytes 98336 | tf_op jit(solution)/shard_map/all_to_all | solution.py:409
  43.3 1.5 %finish.1 = f32[6,32,128]{2,1,0:T(8,128)} custom-call(s32[1,4,8]{2,1,0:T(4,128)} %bitcast.13, f32[256,128]{1,0:T(8,128)S(1)} %bitcast.9, f32[256,128]{1,0:T(8,128)S(1)} %get-tuple-element.8.own_ref, f32[256,128]{1,0:T(8,128)S(1)} %collective-permute-done.2.loan_ref, f32[8,24,128]{2,1,0:T(8,128)S(1)} %all-to-all-done.1.back_ref), custom_call_target="tpu_custom_call" | custom-call | tf_op jit(solution)/shard_map/finish/pallas_call | solution.py:410
Async XLA Ops:
  1.6 7.4 %copy-start = (f32[32,8,128]{2,1,0:T(8,128)S(1)}, f32[32,8,128]{2,1,0:T(8,128)}, u32[]{:S(2)}) copy-start(f32[32,8,128]{2,1,0:T(8,128)} %param.6) | copy-start | bytes 393220
  1.6 14.8 %all-to-all-start = ((f32[8,32,128]{2,1,0:T(8,128)}), f32[8,32,128]{2,1,0:T(8,128)S(1)}, u32[]{:S(2)}, u32[]{:S(2)}) async-start(f32[8,32,128]{2,1,0:T(8,128)} %ship_gather.1), calls=%async_computation | async-start | bytes 262144 | tf_op jit(solution)/shard_map/all_to_all | solution.py:378
  9.0 5.2 %collective-permute-start.1 = (f32[256,128]{1,0:T(8,128)S(1)}, f32[256,128]{1,0:T(8,128)S(1)}, u32[]{:S(2)}, u32[]{:S(2)}) collective-permute-start(f32[256,128]{1,0:T(8,128)S(1)} %bitcast.7), channel_id=1, source_target_pairs={{0,1},{1,0},{2,3},{3,2},{4,5},{5,4},{6,7},{7,6},{8,9},{9,8},{10,11... | collective-permute-start | bytes 393224 | tf_op jit(solution)/shard_map/ppermute | solution.py:380
  11.6 2.6 %collective-permute-start = (s32[128]{0:T(128)}, s32[128]{0:T(128)S(1)}, u32[]{:S(2)}, u32[]{:S(2)}) collective-permute-start(s32[128]{0:T(128)} %plan_tiles.1.list_ref), channel_id=1, source_target_pairs={{0,1},{1,0},{2,3},{3,2},{4,5},{5,4},{6,7},{7,6},{8,9},{9,8},{10,11... | collective-permute-start | bytes 1544 | tf_op jit(solution)/shard_map/ppermute | solution.py:389
  32.9 10.4 %all-to-all-start.1 = ((f32[8,24,128]{2,1,0:T(8,128)}), f32[8,24,128]{2,1,0:T(8,128)S(1)}, u32[]{:S(2)}, u32[]{:S(2)}) async-start(f32[8,24,128]{2,1,0:T(8,128)} %get-tuple-element.10), calls=%async_computation.1 | async-start | bytes 196608 | tf_op jit(solution)/shard_map/all_to_all | solution.py:409
  36.2 1.4 %collective-permute-start.2 = (f32[256,128]{1,0:T(8,128)S(1)}, f32[256,128]{1,0:T(8,128)S(1)}, u32[]{:S(2)}, u32[]{:S(2)}) collective-permute-start(f32[256,128]{1,0:T(8,128)S(1)} %get-tuple-element.9), channel_id=1, source_target_pairs={{0,1},{1,0},{2,3},{3,2},{4,5},{5,4},{6,7},{7,6},{8,9},{9,8},{10,11... | collective-permute-start | bytes 393224 | tf_op jit(solution)/shard_map/ppermute | solution.py:408

commit v3 on v1

--- a/solution.py
+++ b/solution.py
@@ -25,7 +25,7 @@
 PLACES += [{}] * 4
 HEAD = 8
 BATCH = 4
-PREP = 8
+PREP = 16
 
 
 def parts(x):

time: 44.9 us -> 44.4 us (0.989)
  Pallas kernels: 21.5 us -> 15.7 us
  starting transfers between devices: 11.2 us -> 16.8 us
    pallas_call x1, Pallas kernels: 15.6 us -> 11 us  [body(): pl.pallas_call(tile_kernel, out_shape=[pltpu.VMEM(own_sums.shape, F32), j...]
    all_to_all x1, starting transfers between devices: 3.69 us -> 7.93 us  [body(): lax.all_to_all(back, 'brick', split_axis=0, concat_axis=0, tiled=True)]
    pallas_call x1, Pallas kernels: 2.89 us -> 1.62 us  [body(): pl.pallas_call(functools.partial(plan_kernel, leaves), out_shape=tile_lis...]
    ppermute x1, starting transfers between devices: 0.07 us -> 1.22 us  [body(): other_tiles = lax.ppermute(tiles, 'region', partner)]
    all_to_all x1, waiting for transfers between devices: 2.28 us -> 2.73 us  [body(): lax.all_to_all(outgoing, 'brick', split_axis=0, concat_axis=0, tiled=True)]
  transfers between devices with their start and end apart: 5 -> 5, of which waited for: 4 -> 4; matrix products, arithmetic and copies ran while one was open for 0% -> 0% of each run, Pallas kernels for 7% -> 4%
where the time goes in v3:
time: 44.4 us; the launch traced here: 43.9 us
  starting transfers between devices  16.8 us (38%)
  Pallas kernels  15.7 us (35%)
  waiting for transfers between devices  10.7 us (24%)
  between operations  0.68 us (2%)
    pallas_call x1, Pallas kernels, body(): pl.pallas_call(tile_kernel, out_shape=[pltpu.VMEM(own_sums.shape, F32), j...  11 us
    all_to_all x1, starting transfers between devices, body(): lax.all_to_all(back, 'brick', split_axis=0, concat_axis=0, tiled=True)  7.93 us
    all_to_all x1, starting transfers between devices, body(): lax.all_to_all(outgoing, 'brick', split_axis=0, concat_axis=0, tiled=True)  7.41 us
    all_to_all x1, waiting for transfers between devices, body(): lax.all_to_all(back, 'brick', split_axis=0, concat_axis=0, tiled=True)  5.78 us
    all_to_all x1, waiting for transfers between devices, body(): lax.all_to_all(outgoing, 'brick', split_axis=0, concat_axis=0, tiled=True)  2.73 us
    pallas_call x1, Pallas kernels, body(): pl.pallas_call(functools.partial(plan_kernel, leaves), out_shape=tile_lis...  1.62 us
    pallas_call x1, Pallas kernels, body(): pl.pallas_call(gather_kernel, out_shape=jax.ShapeDtypeStruct((bricks, slo...  1.59 us
    pallas_call x1, Pallas kernels, body(): pl.pallas_call(finish_kernel, out_shape=jax.ShapeDtypeStruct((6, leaves,...  1.46 us
  transfers between devices with their start and end apart: 5, of which 4 were waited for; matrix products, arithmetic and copies ran while one was open for 0% of the time, Pallas kernels for 4%

profile of v3, /device:TPU:0, one launch (start us, length us, event | category | flops | bytes accessed | tf_op | source)
XLA Modules:
  0.0 43.9 jit_solution(6068096203178083083)
XLA Ops:
  0.0 1.6 %ship_gather.1 = f32[8,32,128]{2,1,0:T(8,128)} custom-call(s32[1,4,8]{2,1,0:T(4,128)} %bitcast.11, f32[256,128]{1,0:T(8,128)} %bitcast.6), custom_call_target="tpu_custom_call" | custom-call | tf_op jit(solution)/shard_map/ship_gather/pallas_call | solution.py:363
  1.6 0.0 copy-start
  1.6 7.4 %all-to-all-start = ((f32[8,32,128]{2,1,0:T(8,128)}), f32[8,32,128]{2,1,0:T(8,128)S(1)}, u32[]{:S(2)}, u32[]{:S(2)}) async-start(f32[8,32,128]{2,1,0:T(8,128)} %ship_gather.1), calls=%async_computation | async-start | bytes 262144 | tf_op jit(solution)/shard_map/all_to_all | solution.py:370
  9.0 0.0 copy-done
  9.0 0.1 collective-permute-start.1
  9.7 1.6 %plan_tiles.1.list_ref = s32[128]{0:T(128)} custom-call(s32[1,4,8]{2,1,0:T(4,128)} %bitcast.12, s32[1,2,64]{2,1,0:T(2,128)} %bitcast.15, s32[1]{0:T(128)S(6)} %copy.7.count_ref, s32[1,4,2,8]{3,2,1,0:T(2,128)} %bitcast.14, s32[1,4,4]{2,1,0:T(4,128)} %plan_ref.1), custom_call_target="tpu_custom_call" | custom-call | tf_op jit(solution)/shard_map/plan_tiles/pallas_call | solution.py:373
  11.4 1.2 %collective-permute-start = (s32[128]{0:T(128)}, s32[128]{0:T(128)S(1)}, u32[]{:S(2)}, u32[]{:S(2)}) collective-permute-start(s32[128]{0:T(128)} %plan_tiles.1.list_ref), channel_id=1, source_target_pairs={{0,1},{1,0},{2,3},{3,2},{4,5},{5,4},{6,7},{7,6},{8,9},{9,8},{10,11... | collective-permute-start | bytes 1544 | tf_op jit(solution)/shard_map/ppermute | solution.py:381
  12.6 1.0 %collective-permute-done.other_in = s32[128]{0:T(128)S(1)} collective-permute-done((s32[128]{0:T(128)}, s32[128]{0:T(128)S(1)}, u32[]{:S(2)}, u32[]{:S(2)}) %collective-permute-start) | collective-permute-done | bytes 544 | tf_op jit(solution)/shard_map/ppermute | solution.py:381
  13.6 0.0 collective-permute-done.1.guest_ref
  13.6 2.7 %all-to-all-done = f32[8,32,128]{2,1,0:T(8,128)S(1)} async-done(((f32[8,32,128]{2,1,0:T(8,128)}), f32[8,32,128]{2,1,0:T(8,128)S(1)}, u32[]{:S(2)}, u32[]{:S(2)}) %all-to-all-start) | async-done | bytes 131104 | tf_op jit(solution)/shard_map/all_to_all | solution.py:370
  16.4 11.0 %all_tiles.1 = (f32[256,128]{1,0:T(8,128)S(1)}, f32[8,24,128]{2,1,0:T(8,128)}, f32[256,128]{1,0:T(8,128)S(1)}) custom-call(s32[128]{0:T(128)} %plan_tiles.1.list_ref, s32[128]{0:T(128)S(1)} %collective-permute-done.other_in, f32[256,128]{1,0:T(8,128)S(1)} %bitcast.8, f32[256,128]{1,0:T(8,128)S(1)} %bitcast.10, f32[256,128]{1,0:T(8,128)S(1)} %collective-permute-done.1.guest_ref), custom_call_target="tpu_custom_call" | custom-call | tf_op jit(solution)/shard_map/all_tiles/pallas_call | solution.py:382
  27.4 7.9 %all-to-all-start.1 = ((f32[8,24,128]{2,1,0:T(8,128)}), f32[8,24,128]{2,1,0:T(8,128)S(1)}, u32[]{:S(2)}, u32[]{:S(2)}) async-start(f32[8,24,128]{2,1,0:T(8,128)} %get-tuple-element.10), calls=%async_computation.1 | async-start | bytes 196608 | tf_op jit(solution)/shard_map/all_to_all | solution.py:401
  35.3 0.2 collective-permute-start.2
  35.5 1.2 %collective-permute-done.2.loan_ref = f32[256,128]{1,0:T(8,128)S(1)} collective-permute-done((f32[256,128]{1,0:T(8,128)S(1)}, f32[256,128]{1,0:T(8,128)S(1)}, u32[]{:S(2)}, u32[]{:S(2)}) %collective-permute-start.2) | collective-permute-done | bytes 131104 | tf_op jit(solution)/shard_map/ppermute | solution.py:400
  36.7 5.8 %all-to-all-done.1.back_ref = f32[8,24,128]{2,1,0:T(8,128)S(1)} async-done(((f32[8,24,128]{2,1,0:T(8,128)}), f32[8,24,128]{2,1,0:T(8,128)S(1)}, u32[]{:S(2)}, u32[]{:S(2)}) %all-to-all-start.1) | async-done | bytes 98336 | tf_op jit(solution)/shard_map/all_to_all | solution.py:401
  42.5 1.5 %finish.1 = f32[6,32,128]{2,1,0:T(8,128)} custom-call(s32[1,4,8]{2,1,0:T(4,128)} %bitcast.13, f32[256,128]{1,0:T(8,128)S(1)} %bitcast.9, f32[256,128]{1,0:T(8,128)S(1)} %get-tuple-element.8.own_ref, f32[256,128]{1,0:T(8,128)S(1)} %collective-permute-done.2.loan_ref, f32[8,24,128]{2,1,0:T(8,128)S(1)} %all-to-all-done.1.back_ref), custom_call_target="tpu_custom_call" | custom-call | tf_op jit(solution)/shard_map/finish/pallas_call | solution.py:402
Async XLA Ops:
  1.6 7.4 %copy-start = (f32[32,8,128]{2,1,0:T(8,128)S(1)}, f32[32,8,128]{2,1,0:T(8,128)}, u32[]{:S(2)}) copy-start(f32[32,8,128]{2,1,0:T(8,128)} %param.6) | copy-start | bytes 393220
  1.6 14.8 %all-to-all-start = ((f32[8,32,128]{2,1,0:T(8,128)}), f32[8,32,128]{2,1,0:T(8,128)S(1)}, u32[]{:S(2)}, u32[]{:S(2)}) async-start(f32[8,32,128]{2,1,0:T(8,128)} %ship_gather.1), calls=%async_computation | async-start | bytes 262144 | tf_op jit(solution)/shard_map/all_to_all | solution.py:370
  9.0 4.6 %collective-permute-start.1 = (f32[256,128]{1,0:T(8,128)S(1)}, f32[256,128]{1,0:T(8,128)S(1)}, u32[]{:S(2)}, u32[]{:S(2)}) collective-permute-start(f32[256,128]{1,0:T(8,128)S(1)} %bitcast.7), channel_id=1, source_target_pairs={{0,1},{1,0},{2,3},{3,2},{4,5},{5,4},{6,7},{7,6},{8,9},{9,8},{10,11... | collective-permute-start | bytes 393224 | tf_op jit(solution)/shard_map/ppermute | solution.py:372
  11.4 2.2 %collective-permute-start = (s32[128]{0:T(128)}, s32[128]{0:T(128)S(1)}, u32[]{:S(2)}, u32[]{:S(2)}) collective-permute-start(s32[128]{0:T(128)} %plan_tiles.1.list_ref), channel_id=1, source_target_pairs={{0,1},{1,0},{2,3},{3,2},{4,5},{5,4},{6,7},{7,6},{8,9},{9,8},{10,11... | collective-permute-start | bytes 1544 | tf_op jit(solution)/shard_map/ppermute | solution.py:381
  27.4 15.1 %all-to-all-start.1 = ((f32[8,24,128]{2,1,0:T(8,128)}), f32[8,24,128]{2,1,0:T(8,128)S(1)}, u32[]{:S(2)}, u32[]{:S(2)}) async-start(f32[8,24,128]{2,1,0:T(8,128)} %get-tuple-element.10), calls=%async_computation.1 | async-start | bytes 196608 | tf_op jit(solution)/shard_map/all_to_all | solution.py:401
  35.3 1.3 %collective-permute-start.2 = (f32[256,128]{1,0:T(8,128)S(1)}, f32[256,128]{1,0:T(8,128)S(1)}, u32[]{:S(2)}, u32[]{:S(2)}) collective-permute-start(f32[256,128]{1,0:T(8,128)S(1)} %get-tuple-element.9), channel_id=1, source_target_pairs={{0,1},{1,0},{2,3},{3,2},{4,5},{5,4},{6,7},{7,6},{8,9},{9,8},{10,11... | collective-permute-start | bytes 393224 | tf_op jit(solution)/shard_map/ppermute | solution.py:400
